TPU v7x, 256 devices: a whole 4x4x8 slice. The times are simulated.
256 devices in a mesh: tok: 32 (over x, z), head: 8 (over y, core).
Axes of the slice: x: 4, y: 4, z: 8, core: 2. Of those that a mesh axis runs over, the one named last changes fastest.
Arguments:
- queries: bfloat16 [131072, 8, 1024], P('tok', 'head'), as said below
- keys: bfloat16 [131072, 8, 128], P('tok', 'head'), as said below
- basis: float32 [8, 1024, 256], P('head'), may hold values from -0.1875 to 0.1875
Outputs:
- subspace: float32 [8, 1024, 256], P('head')
- keymap: float32 [8, 128, 256], replicated
Inputs may be any that keep to these rules, and one draw needn't show every extreme that they name: `queries`: query features are correlated within a group and share a common part with the keys. `keys`: keys share a common part with the queries of the same tokens.
All inputs are finite; a program needn't handle non-finite values.
Results may differ from a plain program's by a relative error of at most 0.0007.
Values sent between devices are 32-bit elements; how exact they have to be, the bound alone decides.
No kernel may reach another device: no remote copies, remote signals or barrier semaphores. Data moves between devices by JAX's collectives and lax.ppermute only.
A program may use at most 64 MiB of HBM per device.

v0:
```python
import jax
import jax.numpy as jnp
from jax import lax
from jax.experimental import pallas as pl
from jax.experimental.pallas import tpu as pltpu
from jax.sharding import PartitionSpec as P

ridge = 0.1
eps = 1e-06
high = lax.Precision.HIGHEST
f32 = jnp.float32
bf16 = jnp.bfloat16

NX, NZ, NY, NCORE = 4, 8, 4, 2
NQ = 4
STEPS = 8

VMEM_LIMIT = 36 * 1024 * 1024


def dot(a, b, ca, cb, precision=high):
    return lax.dot_general(
        a, b, (((ca,), (cb,)), ((), ())), precision=precision, preferred_element_type=f32
    )


def split(v):
    top = v.astype(bf16)
    return top, (v - top.astype(f32)).astype(bf16)


def dot_split(a, b, ca, cb):
    (ah, al), (bh, bl) = a, b
    return dot(ah, bh, ca, cb, None) + (dot(ah, bl, ca, cb, None) + dot(al, bh, ca, cb, None))


def call(body, outs, scratch, pos, *args):
    spec = pl.BlockSpec(memory_space=pltpu.VMEM)
    many = isinstance(outs, list)
    shapes = [jax.ShapeDtypeStruct(s, f32) for s in (outs if many else [outs])]
    in_specs = [pl.BlockSpec(memory_space=pltpu.SMEM)] + [spec] * len(args)
    result = pl.pallas_call(
        body,
        out_shape=shapes,
        in_specs=in_specs,
        out_specs=[spec] * len(shapes),
        scratch_shapes=scratch,
        compiler_params=pltpu.CompilerParams(vmem_limit_bytes=VMEM_LIMIT),
    )(pos, *args)
    return result if many else result[0]


def inverse_factor_128(read, write):
    tile = (8, 128)
    row = lax.broadcasted_iota(jnp.int32, tile, 0)
    lane = lax.broadcasted_iota(jnp.int32, tile, 1)

    def lanes(v, j):
        return jnp.broadcast_to(v[:, j : j + 1], tile)

    def rows(v, i):
        return jnp.broadcast_to(v[i : i + 1, :], tile)

    def panels(turn, carry):
        left, right = list(carry[:16]), list(carry[16:])
        for p in range(STEPS):
            base = 8 * p
            cols = [lanes(left[p], base + j) for j in range(8)]
            s = [[rows(cols[j], i) for j in range(i + 1)] for i in range(8)]
            r = []
            for j in range(8):
                r.append(lax.rsqrt(s[j][j]))
                for i in range(j + 1, 8):
                    s[i][j] = s[i][j] * r[j]
                for i in range(j + 1, 8):
                    for l in range(j + 1, i + 1):
                        s[i][l] = s[i][l] - s[i][j] * s[l][j]

            def solve(v):
                for j in range(8):
                    v[j] = v[j] * r[j]
                    for i in range(j + 1, 8):
                        v[i] = v[i] - s[i][j] * v[j]
                return v

            ul = solve([rows(left[p], i) for i in range(8)])
            ur = solve([rows(right[p], i) for i in range(8)])
            out = ur[0]
            for i in range(1, 8):
                out = jnp.where(row == i, ur[i], out)
            write(turn * STEPS + p, out)
            for k in range(p + 1, 16):
                c = solve([lanes(left[k], base + j) for j in range(8)])
                for i in range(8):
                    left[k] = left[k] - c[i] * ul[i]
                    right[k] = right[k] - c[i] * ur[i]
        rest = [jnp.zeros(tile, f32)] * STEPS
        left = [pltpu.roll(v, 128 - 8 * STEPS, 1) for v in left[STEPS:]] + rest
        return tuple(left + right[STEPS:] + rest)

    left = [read(r) for r in range(16)]
    right = [jnp.where(lane == row + 8 * r, 1.0, 0.0).astype(f32) for r in range(16)]
    lax.fori_loop(0, 16 // STEPS, panels, tuple(left + right))


def inverse_factor_256(a_ref, li_ref):
    def half(h, carry):
        base = pl.multiple_of(h * 128, 128)

        @pl.when(h == 1)
        def _():
            l21 = dot(a_ref[128:256, 0:128], li_ref[0:128, 0:128], 1, 1)
            a_ref[128:256, 0:128] = l21
            a_ref[128:256, 128:256] = a_ref[128:256, 128:256] - dot(l21, l21, 1, 1)

        def part(r):
            return pl.ds(pl.multiple_of(base + 8 * r, 8), 8), pl.ds(base, 128)

        def write(r, v):
            li_ref[part(r)] = v

        inverse_factor_128(lambda r: a_ref[part(r)], write)
        return carry

    lax.fori_loop(0, 2, half, 0)
    li11, li22 = li_ref[0:128, 0:128], li_ref[128:256, 128:256]
    li_ref[128:256, 0:128] = -dot(li22, dot(a_ref[128:256, 0:128], li11, 1, 0), 1, 0)
    li_ref[0:128, 128:256] = jnp.zeros((128, 128), f32)


def products_call(pos, q, k, b, total):
    tokens, width = q.shape
    features, rank = k.shape[1], b.shape[1]
    tiles = [tokens // 8, tokens // 8, tokens // 4, tokens // 2]
    edges = [sum(tiles[:i]) for i in range(len(tiles) + 1)]
    count = len(tiles)
    side = width // 4
    spans = [slice(side * i, side * i + side) for i in range(4)]
    norm = 1.0 / total

    def body(pos, q_hbm, k_hbm, b_hbm, top, low, cross, trace, o0, o1, o2, o3,
             q, k, b, gram, sems):
        arrivals = []
        for i in range(count):
            part = pl.ds(edges[i], tiles[i])
            pair = [
                pltpu.make_async_copy(q_hbm.at[part], q.at[part], sems.at[2 * i]),
                pltpu.make_async_copy(k_hbm.at[part], k.at[part], sems.at[2 * i + 1]),
            ]
            for copy in pair:
                copy.start()
            arrivals.append(pair)
        basis_copy = pltpu.make_async_copy(b_hbm, b, sems.at[2 * count])
        basis_copy.start()
        for i in range(count):
            for copy in arrivals[i]:
                copy.wait()
            rows = slice(edges[i], edges[i + 1])
            for span in spans:
                part = dot(q[rows, span], q[rows, span.start:], 0, 0, None)
                gram[span, span.start:] = part if i == 0 else gram[span, span.start:] + part
            part = dot(k[rows, :], q[rows, :], 0, 0, None)
            cross[...] = part if i == 0 else cross[...] + part
        cross[...] = cross[...] * norm

        row = lax.broadcasted_iota(jnp.int32, (side, side), 0)
        col = lax.broadcasted_iota(jnp.int32, (side, side), 1)
        diagonal = jnp.zeros((side, side), f32)
        for i in range(4):
            for j in range(i, 4):
                block = gram[spans[i], spans[j]] * norm
                top[spans[i], spans[j]], low[spans[i], spans[j]] = split(block)
                if j == i:
                    diagonal = diagonal + jnp.where(row == col, block, 0.0)
                else:
                    top[spans[j], spans[i]], low[spans[j], spans[i]] = split(block.T)
        total_of = jnp.sum(jnp.sum(diagonal, axis=1, keepdims=True), axis=0, keepdims=True)
        trace[...] = jnp.broadcast_to(total_of, trace.shape)

        basis_copy.wait()
        basis = split(b[...])
        for j, out in enumerate((o0, o1, o2, o3)):
            part = pl.ds(pl.multiple_of(lax.rem(pos[0] + j, NX) * side, side), side)
            out[...] = dot_split((top[part, :], low[part, :]), basis, 1, 0)

    hbm = pl.BlockSpec(memory_space=pltpu.HBM)
    vmem = pl.BlockSpec(memory_space=pltpu.VMEM)
    shape = jax.ShapeDtypeStruct
    return pl.pallas_call(
        body,
        out_shape=[
            shape((width, width), bf16),
            shape((width, width), bf16),
            shape((features, width), f32),
            shape((8, 128), f32),
        ] + [shape((side, rank), f32)] * NX,
        in_specs=[pl.BlockSpec(memory_space=pltpu.SMEM), hbm, hbm, hbm],
        out_specs=[vmem] * (4 + NX),
        scratch_shapes=[
            pltpu.VMEM((tokens, width), bf16),
            pltpu.VMEM((tokens, features), bf16),
            pltpu.VMEM((width, rank), f32),
            pltpu.VMEM((width, width), f32),
            pltpu.SemaphoreType.DMA((2 * count + 1,)),
        ],
        compiler_params=pltpu.CompilerParams(vmem_limit_bytes=VMEM_LIMIT),
    )(pos, *[pltpu.with_memory_space_constraint(v, pltpu.HBM) for v in (q, k, b)])


def sum_and_split(pos, a0, a1, a2, a3, o0, o1, o2, o3, acc):
    acc[...] = (a0[...] + a2[...]) + (a1[...] + a3[...])
    size = acc.shape[0] // NQ
    for j, out in enumerate((o0, o1, o2, o3)):
        start = pl.multiple_of(lax.rem(pos[1] + j, NQ) * size, size)
        out[...] = acc[pl.ds(start, size), :]


def join(pos, a0, a1, a2, a3, out):
    size = a0.shape[0]
    for j, block in enumerate((a0, a1, a2, a3)):
        start = pl.multiple_of(lax.rem(pos[1] + NQ - j, NQ) * size, size)
        out[pl.ds(start, size), :] = block[...]


def subspace_body(pos, s0, s1, s2, s3, cross, trace, top, low, refined, packed, image, inner, li):
    size = s0.shape[0]
    for j, block in enumerate((s0, s1, s2, s3)):
        start = pl.multiple_of(lax.rem(pos[0] + NX - j, NX) * size, size)
        image[pl.ds(start, size), :] = block[...]
    inner[...] = dot(image[...], image[...], 0, 0)
    inverse_factor_256(inner, li)
    basis = dot(image[...], li[...], 1, 1)
    refined[...] = basis
    parts = split(basis)
    product = dot_split((top[...], low[...]), parts, 1, 0)
    small = dot_split(parts, split(product), 0, 0)
    packed[:, 0:128] = small[:, 0:128]
    packed[0:128, 128:256] = jnp.broadcast_to(trace[0:1, :], (128, 128))
    packed[128:256, 128:256] = small[128:256, 128:256]
    packed[:, 256:384] = dot_split(split(cross[...]), parts, 1, 0).T


def sum_over_tok(pos, pieces, out):
    blocks = [pieces[8 * i : 8 * i + 8, :] for i in range(NX * NZ)]
    while len(blocks) > 1:
        blocks = [a + b for a, b in zip(blocks[0::2], blocks[1::2])]
    for i in range(NX * NZ):
        out[8 * i : 8 * i + 8, :] = blocks[0]


def keymap_body(width, pos, joined, out, reduced, li):
    scale = joined[0:1, 128:129] / width + eps
    row = lax.broadcasted_iota(jnp.int32, (256, 256), 0)
    col = lax.broadcasted_iota(jnp.int32, (256, 256), 1)
    identity = jnp.where(row == col, ridge, 0.0).astype(f32)
    reduced[...] = joined[:, 0:256] / scale + identity
    inverse_factor_256(reduced, li)
    rhs = joined[:, 256:384].T
    out[...] = dot(dot(rhs, li[...], 1, 1), li[...], 1, 0)


def place_body(pos, own, other, out):
    for j in range(NY):
        y = lax.rem(pos[2] + NY - j, NY)
        out[NCORE * y + pos[3]] = own[128 * j : 128 * j + 128, :]
        out[NCORE * y + (1 - pos[3])] = other[128 * j : 128 * j + 128, :]


def along_x(value, j):
    pairs = [(x * NZ + z, ((x + j) % NX) * NZ + z) for x in range(NX) for z in range(NZ)]
    return lax.ppermute(value, "tok", pairs)


def along_quad(value, j):
    pairs = [
        (x * NZ + z, x * NZ + z // NQ * NQ + (z + j) % NQ) for x in range(NX) for z in range(NZ)
    ]
    return lax.ppermute(value, "tok", pairs)


def other_quad(value):
    pairs = [(x * NZ + z, x * NZ + (z + NQ) % NZ) for x in range(NX) for z in range(NZ)]
    return lax.ppermute(value, "tok", pairs)


def along_y(value, j):
    pairs = [(y * NCORE + c, ((y + j) % NY) * NCORE + c) for y in range(NY) for c in range(NCORE)]
    return lax.ppermute(value, "head", pairs)


def other_core(value):
    pairs = [(y * NCORE + c, y * NCORE + 1 - c) for y in range(NY) for c in range(NCORE)]
    return lax.ppermute(value, "head", pairs)


def scatter(move, parts):
    return [parts[0]] + [move(parts[j], j) for j in range(1, 4)]


def gather(move, value):
    return [value] + [move(value, j) for j in range(1, 4)]


def on_device(queries, keys, basis):
    q, key, b = queries[:, 0, :], keys[:, 0, :], basis[0]
    width, rank = b.shape
    features = key.shape[1]
    total = q.shape[0] * lax.axis_size("tok")
    tok, head = lax.axis_index("tok"), lax.axis_index("head")
    pos = jnp.stack([tok // NZ, tok % NQ, head // NCORE, head % NCORE]).astype(jnp.int32)

    top, low, cross, trace, *quarters = products_call(pos, q, key, b, total)
    quarter, piece = (width // NX, rank), (width // NX // NQ, rank)
    arrived = scatter(along_x, quarters)
    pieces = call(sum_and_split, [piece] * NQ, [pltpu.VMEM(quarter, f32)], pos, *arrived)
    a0, a1, a2, a3 = scatter(along_quad, pieces)
    half = (a0 + a2) + (a1 + a3)
    whole = half + other_quad(half)
    rows = call(join, quarter, [], pos, *gather(along_quad, whole))

    square = pltpu.VMEM((rank, rank), f32)
    refined, packed = call(
        subspace_body,
        [(width, rank), (rank, rank + features)],
        [pltpu.VMEM((width, rank), f32), square, square],
        pos, *gather(along_x, rows), cross, trace, top, low,
    )
    pieces = lax.all_to_all(packed, "tok", 0, 0, tiled=True)
    sums = call(sum_over_tok, packed.shape, [], pos, pieces)
    joined = lax.all_to_all(sums, "tok", 0, 0, tiled=True)

    def keymap(*refs):
        keymap_body(width, *refs)

    mapped = call(keymap, (features, rank), [square, square], pos, joined)
    own = jnp.concatenate(gather(along_y, mapped), axis=0)
    every_map = call(
        place_body, (NY * NCORE, features, rank), [], pos, own, other_core(own)
    )
    return refined[None], every_map


def solution(mesh):
    placed = (P("tok", "head", None), P("tok", "head", None), P("head", None, None))
    return jax.shard_map(
        on_device,
        mesh=mesh,
        in_specs=placed,
        out_specs=(P("head", None, None), P()),
        check_vma=False,
    )
```

profile of v0, /device:TPU:1, one launch (start us, length us, event | category | flops | bytes accessed | tf_op | source)
XLA Modules:
  0.0 155.0 jit_solution(15598277027203043267)
XLA Ops:
  0.7 0.1 pad_add_fusion.pos.refs_0_
  0.7 11.4 %shard_map.50 = (bf16[1024,1024]{1,0:T(8,128)(2,1)S(1)}, bf16[1024,1024]{1,0:T(8,128)(2,1)S(1)}, f32[128,1024]{1,0:T(8,128)S(1)}, f32[8,128]{1,0:T(8,128)S(1)}, ...) custom-call(s32[4]{0:T(128)S(1)} %pad_add_fusion.pos.refs_0_, ...), custom_call_target="tpu_custom_call" | custom-call | tf_op jit(solution)/shard_map/pallas_call | solution.py:189
  12.2 2.1 %collective-permute-start = (f32[256,256]{1,0:T(8,128)S(1)}, f32[256,256]{1,0:T(8,128)S(1)}, u32[]{:S(2)}, u32[]{:S(2)}) collective-permute-start(f32[256,256]{1,0:T(8,128)S(1)} %get-tuple-element.17), channel_id=1, source_target_pairs={{0,64},{8,72},{16,80},{24,88},{32,96},{40,104},{48,112},{56,120},{... | collective-permute-start | bytes 786440 | tf_op jit(solution)/shard_map/ppermute | solution.py:271
  14.3 2.5 %collective-permute-start.1 = (f32[256,256]{1,0:T(8,128)S(1)}, f32[256,256]{1,0:T(8,128)S(1)}, u32[]{:S(2)}, u32[]{:S(2)}) collective-permute-start(f32[256,256]{1,0:T(8,128)S(1)} %get-tuple-element.18), channel_id=1, source_target_pairs={{0,128},{8,136},{16,144},{24,152},{32,160},{40,168},{48,176},{56,1... | collective-permute-start | bytes 786440 | tf_op jit(solution)/shard_map/ppermute | solution.py:271
  16.8 1.1 collective-permute-start.2
  17.9 1.4 collective-permute-done.a1
  19.3 8.8 %collective-permute-done.1.a2 = f32[256,256]{1,0:T(8,128)S(1)} collective-permute-done((f32[256,256]{1,0:T(8,128)S(1)}, f32[256,256]{1,0:T(8,128)S(1)}, u32[]{:S(2)}, u32[]{:S(2)}) %collective-permute-start.1) | collective-permute-done | bytes 262176 | tf_op jit(solution)/shard_map/ppermute | solution.py:271
  28.1 0.0 collective-permute-done.2.a3
  28.1 0.6 shard_map.51
  28.7 3.1 %collective-permute-start.3 = (f32[64,256]{1,0:T(8,128)S(1)}, f32[64,256]{1,0:T(8,128)S(1)}, u32[]{:S(2)}, u32[]{:S(2)}) collective-permute-start(f32[64,256]{1,0:T(8,128)S(1)} %get-tuple-element.21), channel_id=1, source_target_pairs={{0,16},{8,24},{16,0},{24,8},{32,48},{40,56},{48,32},{56,40},{64,80... | collective-permute-start | bytes 196616 | tf_op jit(solution)/shard_map/ppermute | solution.py:278
  31.8 1.6 %collective-permute-start.4 = (f32[64,256]{1,0:T(8,128)S(1)}, f32[64,256]{1,0:T(8,128)S(1)}, u32[]{:S(2)}, u32[]{:S(2)}) collective-permute-start(f32[64,256]{1,0:T(8,128)S(1)} %get-tuple-element.22), channel_id=1, source_target_pairs={{0,8},{8,16},{16,24},{24,0},{32,40},{40,48},{48,56},{56,32},{64,72... | collective-permute-start | bytes 196616 | tf_op jit(solution)/shard_map/ppermute | solution.py:278
  33.4 1.6 %collective-permute-start.5 = (f32[64,256]{1,0:T(8,128)S(1)}, f32[64,256]{1,0:T(8,128)S(1)}, u32[]{:S(2)}, u32[]{:S(2)}) collective-permute-start(f32[64,256]{1,0:T(8,128)S(1)} %get-tuple-element.23), channel_id=1, source_target_pairs={{0,24},{8,0},{16,8},{24,16},{32,56},{40,32},{48,40},{56,48},{64,88... | collective-permute-start | bytes 196616 | tf_op jit(solution)/shard_map/ppermute | solution.py:278
  35.0 0.0 collective-permute-done.3
  35.0 2.3 %collective-permute-done.4 = f32[64,256]{1,0:T(8,128)S(1)} collective-permute-done((f32[64,256]{1,0:T(8,128)S(1)}, f32[64,256]{1,0:T(8,128)S(1)}, u32[]{:S(2)}, u32[]{:S(2)}) %collective-permute-start.4) | collective-permute-done | bytes 65568 | tf_op jit(solution)/shard_map/ppermute | solution.py:278
  37.3 0.0 collective-permute-done.5
  37.4 5.1 %collective-permute-start.6 = (f32[64,256]{1,0:T(8,128)S(1)}, f32[64,256]{1,0:T(8,128)S(1)}, u32[]{:S(2)}, u32[]{:S(2)}) collective-permute-start(f32[64,256]{1,0:T(8,128)S(1)} %add_add_fusion), channel_id=1, source_target_pairs={{0,32},{8,40},{16,48},{24,56},{32,0},{40,8},{48,16},{56,24},{64,96... | collective-permute-start | bytes 196616 | tf_op jit(solution)/shard_map/ppermute | solution.py:283
  42.4 2.6 %collective-permute-done.6 = f32[64,256]{1,0:T(8,128)S(1)} collective-permute-done((f32[64,256]{1,0:T(8,128)S(1)}, f32[64,256]{1,0:T(8,128)S(1)}, u32[]{:S(2)}, u32[]{:S(2)}) %collective-permute-start.6) | collective-permute-done | bytes 65568 | tf_op jit(solution)/shard_map/ppermute | solution.py:283
  45.1 2.3 %collective-permute-start.9 = (f32[64,256]{1,0:T(8,128)S(1)}, f32[64,256]{1,0:T(8,128)S(1)}, u32[]{:S(2)}, u32[]{:S(2)}) collective-permute-start(f32[64,256]{1,0:T(8,128)S(1)} %add.26.a0), channel_id=1, source_target_pairs={{0,24},{8,0},{16,8},{24,16},{32,56},{40,32},{48,40},{56,48},{64,88... | collective-permute-start | bytes 196616 | tf_op jit(solution)/shard_map/ppermute | solution.py:278
  47.4 0.0 collective-permute-start.8
  47.4 0.4 collective-permute-start.7
  47.8 1.2 collective-permute-done.9.a3
  49.0 3.9 %collective-permute-done.8.a2 = f32[64,256]{1,0:T(8,128)S(1)} collective-permute-done((f32[64,256]{1,0:T(8,128)S(1)}, f32[64,256]{1,0:T(8,128)S(1)}, u32[]{:S(2)}, u32[]{:S(2)}) %collective-permute-start.8) | collective-permute-done | bytes 65568 | tf_op jit(solution)/shard_map/ppermute | solution.py:278
  52.9 0.0 collective-permute-done.7.a1
  53.0 0.6 shard_map.52.s0
  53.5 3.0 %collective-permute-start.12 = (f32[256,256]{1,0:T(8,128)S(1)}, f32[256,256]{1,0:T(8,128)S(1)}, u32[]{:S(2)}, u32[]{:S(2)}) collective-permute-start(f32[256,256]{1,0:T(8,128)S(1)} %shard_map.52.s0), channel_id=1, source_target_pairs={{0,192},{8,200},{16,208},{24,216},{32,224},{40,232},{48,240},{56,2... | collective-permute-start | bytes 786440 | tf_op jit(solution)/shard_map/ppermute | solution.py:271
  56.5 0.8 collective-permute-start.11
  57.3 0.0 collective-permute-start.10
  57.3 6.1 %collective-permute-done.12.s3 = f32[256,256]{1,0:T(8,128)S(1)} collective-permute-done((f32[256,256]{1,0:T(8,128)S(1)}, f32[256,256]{1,0:T(8,128)S(1)}, u32[]{:S(2)}, u32[]{:S(2)}) %collective-permute-start.12) | collective-permute-done | bytes 262176 | tf_op jit(solution)/shard_map/ppermute | solution.py:271
  63.4 0.0 collective-permute-done.11.s2
  63.4 3.5 %collective-permute-done.10.s1 = f32[256,256]{1,0:T(8,128)S(1)} collective-permute-done((f32[256,256]{1,0:T(8,128)S(1)}, f32[256,256]{1,0:T(8,128)S(1)}, u32[]{:S(2)}, u32[]{:S(2)}) %collective-permute-start.10) | collective-permute-done | bytes 262176 | tf_op jit(solution)/shard_map/ppermute | solution.py:271
  66.9 17.8 %shard_map.53 = (f32[1024,256]{1,0:T(8,128)}, f32[256,384]{1,0:T(8,128)S(1)}) custom-call(s32[4]{0:T(128)S(1)} %pad_add_fusion.pos.refs_0_, f32[256,256]{1,0:T(8,128)S(1)} %shard_map.52.s0, f32[256,256]{1,0:T(8,128)S(1)} %collective-permute-done.10.s1, f32[256,256]{1,0:T(8,128)S(1)} %collective-permute-done.11.s2, ...), custom_call_target="tpu_custom_call" | custom-call | tf_op jit(solution)/shard_map/pallas_call | solution.py:42
  84.7 22.1 %all_to_all.22 = f32[32,8,384]{2,1,0:T(8,128)S(1)} all-to-all(f32[32,8,384]{2,1,0:T(8,128)S(1)} %bitcast.15), channel_id=1, replica_groups=mesh['tok'=32,'head'=8] {'tok'}, dimensions={0} | all-to-all | bytes 786432 | tf_op jit(solution)/shard_map/all_to_all | solution.py:328
  106.8 0.6 shard_map.54
  107.4 17.4 %all_to_all.23 = f32[32,8,384]{2,1,0:T(8,128)S(1)} all-to-all(f32[32,8,384]{2,1,0:T(8,128)S(1)} %bitcast.14), channel_id=1, replica_groups=mesh['tok'=32,'head'=8] {'tok'}, dimensions={0} | all-to-all | bytes 786432 | tf_op jit(solution)/shard_map/all_to_all | solution.py:330
  124.8 10.8 %shard_map.55 = f32[128,256]{1,0:T(8,128)S(1)} custom-call(s32[4]{0:T(128)S(1)} %pad_add_fusion.pos.refs_0_, f32[256,384]{1,0:T(8,128)S(1)} %bitcast.12), custom_call_target="tpu_custom_call" | custom-call | tf_op jit(solution)/shard_map/pallas_call | solution.py:42
  135.6 2.8 %collective-permute-start.15 = (f32[128,256]{1,0:T(8,128)S(1)}, f32[128,256]{1,0:T(8,128)S(1)}, u32[]{:S(2)}, u32[]{:S(2)}) collective-permute-start(f32[128,256]{1,0:T(8,128)S(1)} %shard_map.55), channel_id=1, source_target_pairs={{0,6},{1,7},{2,0},{3,1},{4,2},{5,3},{6,4},{7,5},{8,14},{9,15},{10,... | collective-permute-start | bytes 393224 | tf_op jit(solution)/shard_map/ppermute | solution.py:288
  138.3 0.3 collective-permute-start.14
  138.7 0.7 collective-permute-start.13
  139.4 2.3 %collective-permute-done.15 = f32[128,256]{1,0:T(8,128)S(1)} collective-permute-done((f32[128,256]{1,0:T(8,128)S(1)}, f32[128,256]{1,0:T(8,128)S(1)}, u32[]{:S(2)}, u32[]{:S(2)}) %collective-permute-start.15) | collective-permute-done | bytes 131104 | tf_op jit(solution)/shard_map/ppermute | solution.py:288
  141.7 2.1 %collective-permute-done.14 = f32[128,256]{1,0:T(8,128)S(1)} collective-permute-done((f32[128,256]{1,0:T(8,128)S(1)}, f32[128,256]{1,0:T(8,128)S(1)}, u32[]{:S(2)}, u32[]{:S(2)}) %collective-permute-start.14) | collective-permute-done | bytes 131104 | tf_op jit(solution)/shard_map/ppermute | solution.py:288
  143.8 1.3 collective-permute-done.13
  145.1 6.8 %collective-permute-start.16 = (f32[512,256]{1,0:T(8,128)S(1)}, f32[512,256]{1,0:T(8,128)S(1)}, u32[]{:S(2)}, u32[]{:S(2)}) collective-permute-start(f32[512,256]{1,0:T(8,128)S(1)} %pad_maximum_fusion.own), channel_id=1, source_target_pairs={{0,1},{1,0},{2,3},{3,2},{4,5},{5,4},{6,7},{7,6},{8,9},{9,8},{10,11... | collective-permute-start | bytes 1572872 | tf_op jit(solution)/shard_map/ppermute | solution.py:293
  151.9 1.5 collective-permute-done.16.other
  153.4 1.6 %shard_map.56 = f32[8,128,256]{2,1,0:T(8,128)} custom-call(s32[4]{0:T(128)S(1)} %pad_add_fusion.pos.refs_0_, f32[512,256]{1,0:T(8,128)S(1)} %pad_maximum_fusion.own, f32[512,256]{1,0:T(8,128)S(1)} %collective-permute-done.16.other), custom_call_target="tpu_custom_call" | custom-call | tf_op jit(solution)/shard_map/pallas_call | solution.py:42
  (3 shorter events, 0.1 us)
Async XLA Ops:
  12.2 7.2 %collective-permute-start = (f32[256,256]{1,0:T(8,128)S(1)}, f32[256,256]{1,0:T(8,128)S(1)}, u32[]{:S(2)}, u32[]{:S(2)}) collective-permute-start(f32[256,256]{1,0:T(8,128)S(1)} %get-tuple-element.17), channel_id=1, source_target_pairs={{0,64},{8,72},{16,80},{24,88},{32,96},{40,104},{48,112},{56,120},{... | collective-permute-start | bytes 786440 | tf_op jit(solution)/shard_map/ppermute | solution.py:271
  14.3 13.8 %collective-permute-start.1 = (f32[256,256]{1,0:T(8,128)S(1)}, f32[256,256]{1,0:T(8,128)S(1)}, u32[]{:S(2)}, u32[]{:S(2)}) collective-permute-start(f32[256,256]{1,0:T(8,128)S(1)} %get-tuple-element.18), channel_id=1, source_target_pairs={{0,128},{8,136},{16,144},{24,152},{32,160},{40,168},{48,176},{56,1... | collective-permute-start | bytes 786440 | tf_op jit(solution)/shard_map/ppermute | solution.py:271
  16.8 11.3 %collective-permute-start.2 = (f32[256,256]{1,0:T(8,128)S(1)}, f32[256,256]{1,0:T(8,128)S(1)}, u32[]{:S(2)}, u32[]{:S(2)}) collective-permute-start(f32[256,256]{1,0:T(8,128)S(1)} %get-tuple-element.19), channel_id=1, source_target_pairs={{0,192},{8,200},{16,208},{24,216},{32,224},{40,232},{48,240},{56,2... | collective-permute-start | bytes 786440 | tf_op jit(solution)/shard_map/ppermute | solution.py:271
  28.7 6.3 %collective-permute-start.3 = (f32[64,256]{1,0:T(8,128)S(1)}, f32[64,256]{1,0:T(8,128)S(1)}, u32[]{:S(2)}, u32[]{:S(2)}) collective-permute-start(f32[64,256]{1,0:T(8,128)S(1)} %get-tuple-element.21), channel_id=1, source_target_pairs={{0,16},{8,24},{16,0},{24,8},{32,48},{40,56},{48,32},{56,40},{64,80... | collective-permute-start | bytes 196616 | tf_op jit(solution)/shard_map/ppermute | solution.py:278
  31.8 5.6 %collective-permute-start.4 = (f32[64,256]{1,0:T(8,128)S(1)}, f32[64,256]{1,0:T(8,128)S(1)}, u32[]{:S(2)}, u32[]{:S(2)}) collective-permute-start(f32[64,256]{1,0:T(8,128)S(1)} %get-tuple-element.22), channel_id=1, source_target_pairs={{0,8},{8,16},{16,24},{24,0},{32,40},{40,48},{48,56},{56,32},{64,72... | collective-permute-start | bytes 196616 | tf_op jit(solution)/shard_map/ppermute | solution.py:278
  33.4 3.9 %collective-permute-start.5 = (f32[64,256]{1,0:T(8,128)S(1)}, f32[64,256]{1,0:T(8,128)S(1)}, u32[]{:S(2)}, u32[]{:S(2)}) collective-permute-start(f32[64,256]{1,0:T(8,128)S(1)} %get-tuple-element.23), channel_id=1, source_target_pairs={{0,24},{8,0},{16,8},{24,16},{32,56},{40,32},{48,40},{56,48},{64,88... | collective-permute-start | bytes 196616 | tf_op jit(solution)/shard_map/ppermute | solution.py:278
  37.4 7.7 %collective-permute-start.6 = (f32[64,256]{1,0:T(8,128)S(1)}, f32[64,256]{1,0:T(8,128)S(1)}, u32[]{:S(2)}, u32[]{:S(2)}) collective-permute-start(f32[64,256]{1,0:T(8,128)S(1)} %add_add_fusion), channel_id=1, source_target_pairs={{0,32},{8,40},{16,48},{24,56},{32,0},{40,8},{48,16},{56,24},{64,96... | collective-permute-start | bytes 196616 | tf_op jit(solution)/shard_map/ppermute | solution.py:283
  45.1 3.9 %collective-permute-start.9 = (f32[64,256]{1,0:T(8,128)S(1)}, f32[64,256]{1,0:T(8,128)S(1)}, u32[]{:S(2)}, u32[]{:S(2)}) collective-permute-start(f32[64,256]{1,0:T(8,128)S(1)} %add.26.a0), channel_id=1, source_target_pairs={{0,24},{8,0},{16,8},{24,16},{32,56},{40,32},{48,40},{56,48},{64,88... | collective-permute-start | bytes 196616 | tf_op jit(solution)/shard_map/ppermute | solution.py:278
  47.4 5.5 %collective-permute-start.8 = (f32[64,256]{1,0:T(8,128)S(1)}, f32[64,256]{1,0:T(8,128)S(1)}, u32[]{:S(2)}, u32[]{:S(2)}) collective-permute-start(f32[64,256]{1,0:T(8,128)S(1)} %add.26.a0), channel_id=1, source_target_pairs={{0,16},{8,24},{16,0},{24,8},{32,48},{40,56},{48,32},{56,40},{64,80... | collective-permute-start | bytes 196616 | tf_op jit(solution)/shard_map/ppermute | solution.py:278
  47.4 5.5 %collective-permute-start.7 = (f32[64,256]{1,0:T(8,128)S(1)}, f32[64,256]{1,0:T(8,128)S(1)}, u32[]{:S(2)}, u32[]{:S(2)}) collective-permute-start(f32[64,256]{1,0:T(8,128)S(1)} %add.26.a0), channel_id=1, source_target_pairs={{0,8},{8,16},{16,24},{24,0},{32,40},{40,48},{48,56},{56,32},{64,72... | collective-permute-start | bytes 196616 | tf_op jit(solution)/shard_map/ppermute | solution.py:278
  53.5 9.9 %collective-permute-start.12 = (f32[256,256]{1,0:T(8,128)S(1)}, f32[256,256]{1,0:T(8,128)S(1)}, u32[]{:S(2)}, u32[]{:S(2)}) collective-permute-start(f32[256,256]{1,0:T(8,128)S(1)} %shard_map.52.s0), channel_id=1, source_target_pairs={{0,192},{8,200},{16,208},{24,216},{32,224},{40,232},{48,240},{56,2... | collective-permute-start | bytes 786440 | tf_op jit(solution)/shard_map/ppermute | solution.py:271
  56.5 6.9 %collective-permute-start.11 = (f32[256,256]{1,0:T(8,128)S(1)}, f32[256,256]{1,0:T(8,128)S(1)}, u32[]{:S(2)}, u32[]{:S(2)}) collective-permute-start(f32[256,256]{1,0:T(8,128)S(1)} %shard_map.52.s0), channel_id=1, source_target_pairs={{0,128},{8,136},{16,144},{24,152},{32,160},{40,168},{48,176},{56,1... | collective-permute-start | bytes 786440 | tf_op jit(solution)/shard_map/ppermute | solution.py:271
  57.3 9.7 %collective-permute-start.10 = (f32[256,256]{1,0:T(8,128)S(1)}, f32[256,256]{1,0:T(8,128)S(1)}, u32[]{:S(2)}, u32[]{:S(2)}) collective-permute-start(f32[256,256]{1,0:T(8,128)S(1)} %shard_map.52.s0), channel_id=1, source_target_pairs={{0,64},{8,72},{16,80},{24,88},{32,96},{40,104},{48,112},{56,120},{... | collective-permute-start | bytes 786440 | tf_op jit(solution)/shard_map/ppermute | solution.py:271
  135.6 6.1 %collective-permute-start.15 = (f32[128,256]{1,0:T(8,128)S(1)}, f32[128,256]{1,0:T(8,128)S(1)}, u32[]{:S(2)}, u32[]{:S(2)}) collective-permute-start(f32[128,256]{1,0:T(8,128)S(1)} %shard_map.55), channel_id=1, source_target_pairs={{0,6},{1,7},{2,0},{3,1},{4,2},{5,3},{6,4},{7,5},{8,14},{9,15},{10,... | collective-permute-start | bytes 393224 | tf_op jit(solution)/shard_map/ppermute | solution.py:288
  138.3 5.4 %collective-permute-start.14 = (f32[128,256]{1,0:T(8,128)S(1)}, f32[128,256]{1,0:T(8,128)S(1)}, u32[]{:S(2)}, u32[]{:S(2)}) collective-permute-start(f32[128,256]{1,0:T(8,128)S(1)} %shard_map.55), channel_id=1, source_target_pairs={{0,4},{1,5},{2,6},{3,7},{4,0},{5,1},{6,2},{7,3},{8,12},{9,13},{10,... | collective-permute-start | bytes 393224 | tf_op jit(solution)/shard_map/ppermute | solution.py:288
  138.7 6.4 %collective-permute-start.13 = (f32[128,256]{1,0:T(8,128)S(1)}, f32[128,256]{1,0:T(8,128)S(1)}, u32[]{:S(2)}, u32[]{:S(2)}) collective-permute-start(f32[128,256]{1,0:T(8,128)S(1)} %shard_map.55), channel_id=1, source_target_pairs={{0,2},{1,3},{2,4},{3,5},{4,6},{5,7},{6,0},{7,1},{8,10},{9,11},{10,... | collective-permute-start | bytes 393224 | tf_op jit(solution)/shard_map/ppermute | solution.py:288
  145.1 8.3 %collective-permute-start.16 = (f32[512,256]{1,0:T(8,128)S(1)}, f32[512,256]{1,0:T(8,128)S(1)}, u32[]{:S(2)}, u32[]{:S(2)}) collective-permute-start(f32[512,256]{1,0:T(8,128)S(1)} %pad_maximum_fusion.own), channel_id=1, source_target_pairs={{0,1},{1,0},{2,3},{3,2},{4,5},{5,4},{6,7},{7,6},{8,9},{9,8},{10,11... | collective-permute-start | bytes 1572872 | tf_op jit(solution)/shard_map/ppermute | solution.py:293
where the time goes:
time: 155 us
  Pallas kernels  43.3 us (28%)
  blocking collectives  39.5 us (25%)
  waiting for transfers between devices  37.1 us (24%)
  starting transfers between devices  34.2 us (22%)
    pallas_call x6, Pallas kernels, call(): pl.pallas_call(body, out_shape=shapes, in_specs=in_specs, out_specs=[spec...  31.9 us
    all_to_all x1, blocking collectives, on_device(): pieces = lax.all_to_all(packed, 'tok', 0, 0, tiled=True)  22.1 us
    ppermute x6, waiting for transfers between devices, along_x(): return lax.ppermute(value, 'tok', pairs)  19.8 us
    all_to_all x1, blocking collectives, on_device(): joined = lax.all_to_all(sums, 'tok', 0, 0, tiled=True)  17.4 us
    pallas_call x1, Pallas kernels, products_call(): pl.pallas_call(body, out_shape=[shape((width, width), bf16), shape((width...  11.4 us
    ppermute x6, starting transfers between devices, along_x(): return lax.ppermute(value, 'tok', pairs)  9.47 us
    ppermute x6, starting transfers between devices, along_quad(): return lax.ppermute(value, 'tok', pairs)  9.05 us
    ppermute x6, waiting for transfers between devices, along_quad(): return lax.ppermute(value, 'tok', pairs)  7.41 us
  transfers between devices with their start and end apart: 17, of which 12 were waited for; matrix products, arithmetic and copies ran while one was open for 0% of the time, Pallas kernels for 0%

commit v1 on v0

--- a/solution.py
+++ b/solution.py
@@ -50,7 +50,7 @@
     return result if many else result[0]
 
 
-def inverse_factor_128(read, write):
+def inverse_factor_128(read, write, buf):
     tile = (8, 128)
     row = lax.broadcasted_iota(jnp.int32, tile, 0)
     lane = lax.broadcasted_iota(jnp.int32, tile, 1)
@@ -65,8 +65,13 @@
         left, right = list(carry[:16]), list(carry[16:])
         for p in range(STEPS):
             base = 8 * p
-            cols = [lanes(left[p], base + j) for j in range(8)]
-            s = [[rows(cols[j], i) for j in range(i + 1)] for i in range(8)]
+            slot = 64 * (p % 2)
+            for j in range(8):
+                buf[slot + 8 * j : slot + 8 * j + 8, :] = lanes(left[p], base + j)
+            s = [
+                [buf[pl.ds(slot + 8 * j + i, 8, stride=0), :] for j in range(i + 1)]
+                for i in range(8)
+            ]
             r = []
             for j in range(8):
                 r.append(lax.rsqrt(s[j][j]))
@@ -103,15 +108,15 @@
     lax.fori_loop(0, 16 // STEPS, panels, tuple(left + right))
 
 
-def inverse_factor_256(a_ref, li_ref):
+def inverse_factor_256(a_ref, li_ref, buf):
     def half(h, carry):
         base = pl.multiple_of(h * 128, 128)
 
         @pl.when(h == 1)
         def _():
-            l21 = dot(a_ref[128:256, 0:128], li_ref[0:128, 0:128], 1, 1)
+            l21 = dot(a_ref[128:256, 0:128], li_ref[0:128, 0:128].T, 1, 0)
             a_ref[128:256, 0:128] = l21
-            a_ref[128:256, 128:256] = a_ref[128:256, 128:256] - dot(l21, l21, 1, 1)
+            a_ref[128:256, 128:256] = a_ref[128:256, 128:256] - dot(l21, l21.T, 1, 0)
 
         def part(r):
             return pl.ds(pl.multiple_of(base + 8 * r, 8), 8), pl.ds(base, 128)
@@ -119,7 +124,7 @@
         def write(r, v):
             li_ref[part(r)] = v
 
-        inverse_factor_128(lambda r: a_ref[part(r)], write)
+        inverse_factor_128(lambda r: a_ref[part(r)], write, buf)
         return carry
 
     lax.fori_loop(0, 2, half, 0)
@@ -222,14 +227,15 @@
         out[pl.ds(start, size), :] = block[...]
 
 
-def subspace_body(pos, s0, s1, s2, s3, cross, trace, top, low, refined, packed, image, inner, li):
+def subspace_body(pos, s0, s1, s2, s3, cross, trace, top, low, refined, packed, image, inner, li,
+                  buf):
     size = s0.shape[0]
     for j, block in enumerate((s0, s1, s2, s3)):
         start = pl.multiple_of(lax.rem(pos[0] + NX - j, NX) * size, size)
         image[pl.ds(start, size), :] = block[...]
     inner[...] = dot(image[...], image[...], 0, 0)
-    inverse_factor_256(inner, li)
-    basis = dot(image[...], li[...], 1, 1)
+    inverse_factor_256(inner, li, buf)
+    basis = dot(image[...], li[...].T, 1, 0)
     refined[...] = basis
     parts = split(basis)
     product = dot_split((top[...], low[...]), parts, 1, 0)
@@ -248,15 +254,15 @@
         out[8 * i : 8 * i + 8, :] = blocks[0]
 
 
-def keymap_body(width, pos, joined, out, reduced, li):
+def keymap_body(width, pos, joined, out, reduced, li, buf):
     scale = joined[0:1, 128:129] / width + eps
     row = lax.broadcasted_iota(jnp.int32, (256, 256), 0)
     col = lax.broadcasted_iota(jnp.int32, (256, 256), 1)
     identity = jnp.where(row == col, ridge, 0.0).astype(f32)
     reduced[...] = joined[:, 0:256] / scale + identity
-    inverse_factor_256(reduced, li)
+    inverse_factor_256(reduced, li, buf)
     rhs = joined[:, 256:384].T
-    out[...] = dot(dot(rhs, li[...], 1, 1), li[...], 1, 0)
+    out[...] = dot(dot(rhs, li[...].T, 1, 0), li[...], 1, 0)
 
 
 def place_body(pos, own, other, out):
@@ -318,11 +324,11 @@
     whole = half + other_quad(half)
     rows = call(join, quarter, [], pos, *gather(along_quad, whole))
 
-    square = pltpu.VMEM((rank, rank), f32)
+    square, spread = pltpu.VMEM((rank, rank), f32), pltpu.VMEM((128, 128), f32)
     refined, packed = call(
         subspace_body,
         [(width, rank), (rank, rank + features)],
-        [pltpu.VMEM((width, rank), f32), square, square],
+        [pltpu.VMEM((width, rank), f32), square, square, spread],
         pos, *gather(along_x, rows), cross, trace, top, low,
     )
     pieces = lax.all_to_all(packed, "tok", 0, 0, tiled=True)
@@ -332,7 +338,7 @@
     def keymap(*refs):
         keymap_body(width, *refs)
 
-    mapped = call(keymap, (features, rank), [square, square], pos, joined)
+    mapped = call(keymap, (features, rank), [square, square, spread], pos, joined)
     own = jnp.concatenate(gather(along_y, mapped), axis=0)
     every_map = call(
         place_body, (NY * NCORE, features, rank), [], pos, own, other_core(own)

time: 155 us -> 153 us (0.987)
  Pallas kernels: 43.3 us -> 41.4 us
    pallas_call x6, Pallas kernels: 31.9 us -> 30 us  [call(): pl.pallas_call(body, out_shape=shapes, in_specs=in_specs, out_specs=[spec...]
where the time goes in v1:
time: 153 us
  Pallas kernels  41.4 us (27%)
  blocking collectives  39.3 us (26%)
  waiting for transfers between devices  37.1 us (24%)
  starting transfers between devices  34.2 us (22%)
    pallas_call x6, Pallas kernels, call(): pl.pallas_call(body, out_shape=shapes, in_specs=in_specs, out_specs=[spec...  30 us
    all_to_all x1, blocking collectives, on_device(): pieces = lax.all_to_all(packed, 'tok', 0, 0, tiled=True)  21.9 us
    ppermute x6, waiting for transfers between devices, along_x(): return lax.ppermute(value, 'tok', pairs)  19.8 us
    all_to_all x1, blocking collectives, on_device(): joined = lax.all_to_all(sums, 'tok', 0, 0, tiled=True)  17.4 us
    pallas_call x1, Pallas kernels, products_call(): pl.pallas_call(body, out_shape=[shape((width, width), bf16), shape((width...  11.4 us
    ppermute x6, starting transfers between devices, along_x(): return lax.ppermute(value, 'tok', pairs)  9.47 us
    ppermute x6, starting transfers between devices, along_quad(): return lax.ppermute(value, 'tok', pairs)  9.05 us
    ppermute x6, waiting for transfers between devices, along_quad(): return lax.ppermute(value, 'tok', pairs)  7.41 us
  transfers between devices with their start and end apart: 17, of which 12 were waited for; matrix products, arithmetic and copies ran while one was open for 0% of the time, Pallas kernels for 0%

profile of v1, /device:TPU:1, one launch (start us, length us, event | category | flops | bytes accessed | tf_op | source)
XLA Modules:
  0.0 152.9 jit_solution(743032880350928406)
XLA Ops:
  0.7 0.1 pad_add_fusion.pos.refs_0_
  0.7 11.4 %shard_map.50 = (bf16[1024,1024]{1,0:T(8,128)(2,1)S(1)}, bf16[1024,1024]{1,0:T(8,128)(2,1)S(1)}, f32[128,1024]{1,0:T(8,128)S(1)}, f32[8,128]{1,0:T(8,128)S(1)}, ...) custom-call(s32[4]{0:T(128)S(1)} %pad_add_fusion.pos.refs_0_, ...), custom_call_target="tpu_custom_call" | custom-call | tf_op jit(solution)/shard_map/pallas_call | solution.py:194
  12.2 2.1 %collective-permute-start = (f32[256,256]{1,0:T(8,128)S(1)}, f32[256,256]{1,0:T(8,128)S(1)}, u32[]{:S(2)}, u32[]{:S(2)}) collective-permute-start(f32[256,256]{1,0:T(8,128)S(1)} %get-tuple-element.17), channel_id=1, source_target_pairs={{0,64},{8,72},{16,80},{24,88},{32,96},{40,104},{48,112},{56,120},{... | collective-permute-start | bytes 786440 | tf_op jit(solution)/shard_map/ppermute | solution.py:277
  14.3 2.5 %collective-permute-start.1 = (f32[256,256]{1,0:T(8,128)S(1)}, f32[256,256]{1,0:T(8,128)S(1)}, u32[]{:S(2)}, u32[]{:S(2)}) collective-permute-start(f32[256,256]{1,0:T(8,128)S(1)} %get-tuple-element.18), channel_id=1, source_target_pairs={{0,128},{8,136},{16,144},{24,152},{32,160},{40,168},{48,176},{56,1... | collective-permute-start | bytes 786440 | tf_op jit(solution)/shard_map/ppermute | solution.py:277
  16.8 1.1 collective-permute-start.2
  17.9 1.4 collective-permute-done.a1
  19.3 8.8 %collective-permute-done.1.a2 = f32[256,256]{1,0:T(8,128)S(1)} collective-permute-done((f32[256,256]{1,0:T(8,128)S(1)}, f32[256,256]{1,0:T(8,128)S(1)}, u32[]{:S(2)}, u32[]{:S(2)}) %collective-permute-start.1) | collective-permute-done | bytes 262176 | tf_op jit(solution)/shard_map/ppermute | solution.py:277
  28.1 0.0 collective-permute-done.2.a3
  28.1 0.6 shard_map.51
  28.7 3.1 %collective-permute-start.3 = (f32[64,256]{1,0:T(8,128)S(1)}, f32[64,256]{1,0:T(8,128)S(1)}, u32[]{:S(2)}, u32[]{:S(2)}) collective-permute-start(f32[64,256]{1,0:T(8,128)S(1)} %get-tuple-element.21), channel_id=1, source_target_pairs={{0,16},{8,24},{16,0},{24,8},{32,48},{40,56},{48,32},{56,40},{64,80... | collective-permute-start | bytes 196616 | tf_op jit(solution)/shard_map/ppermute | solution.py:284
  31.8 1.6 %collective-permute-start.4 = (f32[64,256]{1,0:T(8,128)S(1)}, f32[64,256]{1,0:T(8,128)S(1)}, u32[]{:S(2)}, u32[]{:S(2)}) collective-permute-start(f32[64,256]{1,0:T(8,128)S(1)} %get-tuple-element.22), channel_id=1, source_target_pairs={{0,8},{8,16},{16,24},{24,0},{32,40},{40,48},{48,56},{56,32},{64,72... | collective-permute-start | bytes 196616 | tf_op jit(solution)/shard_map/ppermute | solution.py:284
  33.4 1.6 %collective-permute-start.5 = (f32[64,256]{1,0:T(8,128)S(1)}, f32[64,256]{1,0:T(8,128)S(1)}, u32[]{:S(2)}, u32[]{:S(2)}) collective-permute-start(f32[64,256]{1,0:T(8,128)S(1)} %get-tuple-element.23), channel_id=1, source_target_pairs={{0,24},{8,0},{16,8},{24,16},{32,56},{40,32},{48,40},{56,48},{64,88... | collective-permute-start | bytes 196616 | tf_op jit(solution)/shard_map/ppermute | solution.py:284
  35.0 0.0 collective-permute-done.3
  35.0 2.3 %collective-permute-done.4 = f32[64,256]{1,0:T(8,128)S(1)} collective-permute-done((f32[64,256]{1,0:T(8,128)S(1)}, f32[64,256]{1,0:T(8,128)S(1)}, u32[]{:S(2)}, u32[]{:S(2)}) %collective-permute-start.4) | collective-permute-done | bytes 65568 | tf_op jit(solution)/shard_map/ppermute | solution.py:284
  37.3 0.0 collective-permute-done.5
  37.4 5.1 %collective-permute-start.6 = (f32[64,256]{1,0:T(8,128)S(1)}, f32[64,256]{1,0:T(8,128)S(1)}, u32[]{:S(2)}, u32[]{:S(2)}) collective-permute-start(f32[64,256]{1,0:T(8,128)S(1)} %add_add_fusion), channel_id=1, source_target_pairs={{0,32},{8,40},{16,48},{24,56},{32,0},{40,8},{48,16},{56,24},{64,96... | collective-permute-start | bytes 196616 | tf_op jit(solution)/shard_map/ppermute | solution.py:289
  42.4 2.6 %collective-permute-done.6 = f32[64,256]{1,0:T(8,128)S(1)} collective-permute-done((f32[64,256]{1,0:T(8,128)S(1)}, f32[64,256]{1,0:T(8,128)S(1)}, u32[]{:S(2)}, u32[]{:S(2)}) %collective-permute-start.6) | collective-permute-done | bytes 65568 | tf_op jit(solution)/shard_map/ppermute | solution.py:289
  45.1 2.3 %collective-permute-start.9 = (f32[64,256]{1,0:T(8,128)S(1)}, f32[64,256]{1,0:T(8,128)S(1)}, u32[]{:S(2)}, u32[]{:S(2)}) collective-permute-start(f32[64,256]{1,0:T(8,128)S(1)} %add.26.a0), channel_id=1, source_target_pairs={{0,24},{8,0},{16,8},{24,16},{32,56},{40,32},{48,40},{56,48},{64,88... | collective-permute-start | bytes 196616 | tf_op jit(solution)/shard_map/ppermute | solution.py:284
  47.4 0.0 collective-permute-start.8
  47.4 0.4 collective-permute-start.7
  47.8 1.2 collective-permute-done.9.a3
  49.0 3.9 %collective-permute-done.8.a2 = f32[64,256]{1,0:T(8,128)S(1)} collective-permute-done((f32[64,256]{1,0:T(8,128)S(1)}, f32[64,256]{1,0:T(8,128)S(1)}, u32[]{:S(2)}, u32[]{:S(2)}) %collective-permute-start.8) | collective-permute-done | bytes 65568 | tf_op jit(solution)/shard_map/ppermute | solution.py:284
  52.9 0.0 collective-permute-done.7.a1
  53.0 0.6 shard_map.52.s0
  53.5 3.0 %collective-permute-start.12 = (f32[256,256]{1,0:T(8,128)S(1)}, f32[256,256]{1,0:T(8,128)S(1)}, u32[]{:S(2)}, u32[]{:S(2)}) collective-permute-start(f32[256,256]{1,0:T(8,128)S(1)} %shard_map.52.s0), channel_id=1, source_target_pairs={{0,192},{8,200},{16,208},{24,216},{32,224},{40,232},{48,240},{56,2... | collective-permute-start | bytes 786440 | tf_op jit(solution)/shard_map/ppermute | solution.py:277
  56.5 0.8 collective-permute-start.11
  57.3 0.0 collective-permute-start.10
  57.3 6.1 %collective-permute-done.12.s3 = f32[256,256]{1,0:T(8,128)S(1)} collective-permute-done((f32[256,256]{1,0:T(8,128)S(1)}, f32[256,256]{1,0:T(8,128)S(1)}, u32[]{:S(2)}, u32[]{:S(2)}) %collective-permute-start.12) | collective-permute-done | bytes 262176 | tf_op jit(solution)/shard_map/ppermute | solution.py:277
  63.4 0.0 collective-permute-done.11.s2
  63.4 3.5 %collective-permute-done.10.s1 = f32[256,256]{1,0:T(8,128)S(1)} collective-permute-done((f32[256,256]{1,0:T(8,128)S(1)}, f32[256,256]{1,0:T(8,128)S(1)}, u32[]{:S(2)}, u32[]{:S(2)}) %collective-permute-start.10) | collective-permute-done | bytes 262176 | tf_op jit(solution)/shard_map/ppermute | solution.py:277
  66.9 16.8 %shard_map.53 = (f32[1024,256]{1,0:T(8,128)}, f32[256,384]{1,0:T(8,128)S(1)}) custom-call(s32[4]{0:T(128)S(1)} %pad_add_fusion.pos.refs_0_, f32[256,256]{1,0:T(8,128)S(1)} %shard_map.52.s0, f32[256,256]{1,0:T(8,128)S(1)} %collective-permute-done.10.s1, f32[256,256]{1,0:T(8,128)S(1)} %collective-permute-done.11.s2, ...), custom_call_target="tpu_custom_call" | custom-call | tf_op jit(solution)/shard_map/pallas_call | solution.py:42
  83.7 21.9 %all_to_all.22 = f32[32,8,384]{2,1,0:T(8,128)S(1)} all-to-all(f32[32,8,384]{2,1,0:T(8,128)S(1)} %bitcast.15), channel_id=1, replica_groups=mesh['tok'=32,'head'=8] {'tok'}, dimensions={0} | all-to-all | bytes 786432 | tf_op jit(solution)/shard_map/all_to_all | solution.py:334
  105.6 0.6 shard_map.54
  106.2 17.4 %all_to_all.23 = f32[32,8,384]{2,1,0:T(8,128)S(1)} all-to-all(f32[32,8,384]{2,1,0:T(8,128)S(1)} %bitcast.14), channel_id=1, replica_groups=mesh['tok'=32,'head'=8] {'tok'}, dimensions={0} | all-to-all | bytes 786432 | tf_op jit(solution)/shard_map/all_to_all | solution.py:336
  123.6 9.8 %shard_map.55 = f32[128,256]{1,0:T(8,128)S(1)} custom-call(s32[4]{0:T(128)S(1)} %pad_add_fusion.pos.refs_0_, f32[256,384]{1,0:T(8,128)S(1)} %bitcast.12), custom_call_target="tpu_custom_call" | custom-call | tf_op jit(solution)/shard_map/pallas_call | solution.py:42
  133.5 2.8 %collective-permute-start.15 = (f32[128,256]{1,0:T(8,128)S(1)}, f32[128,256]{1,0:T(8,128)S(1)}, u32[]{:S(2)}, u32[]{:S(2)}) collective-permute-start(f32[128,256]{1,0:T(8,128)S(1)} %shard_map.55), channel_id=1, source_target_pairs={{0,6},{1,7},{2,0},{3,1},{4,2},{5,3},{6,4},{7,5},{8,14},{9,15},{10,... | collective-permute-start | bytes 393224 | tf_op jit(solution)/shard_map/ppermute | solution.py:294
  136.2 0.3 collective-permute-start.14
  136.6 0.7 collective-permute-start.13
  137.3 2.3 %collective-permute-done.15 = f32[128,256]{1,0:T(8,128)S(1)} collective-permute-done((f32[128,256]{1,0:T(8,128)S(1)}, f32[128,256]{1,0:T(8,128)S(1)}, u32[]{:S(2)}, u32[]{:S(2)}) %collective-permute-start.15) | collective-permute-done | bytes 131104 | tf_op jit(solution)/shard_map/ppermute | solution.py:294
  139.5 2.1 %collective-permute-done.14 = f32[128,256]{1,0:T(8,128)S(1)} collective-permute-done((f32[128,256]{1,0:T(8,128)S(1)}, f32[128,256]{1,0:T(8,128)S(1)}, u32[]{:S(2)}, u32[]{:S(2)}) %collective-permute-start.14) | collective-permute-done | bytes 131104 | tf_op jit(solution)/shard_map/ppermute | solution.py:294
  141.6 1.3 collective-permute-done.13
  143.0 6.8 %collective-permute-start.16 = (f32[512,256]{1,0:T(8,128)S(1)}, f32[512,256]{1,0:T(8,128)S(1)}, u32[]{:S(2)}, u32[]{:S(2)}) collective-permute-start(f32[512,256]{1,0:T(8,128)S(1)} %pad_maximum_fusion.own), channel_id=1, source_target_pairs={{0,1},{1,0},{2,3},{3,2},{4,5},{5,4},{6,7},{7,6},{8,9},{9,8},{10,11... | collective-permute-start | bytes 1572872 | tf_op jit(solution)/shard_map/ppermute | solution.py:299
  149.8 1.5 %collective-permute-done.16.other = f32[512,256]{1,0:T(8,128)S(1)} collective-permute-done((f32[512,256]{1,0:T(8,128)S(1)}, f32[512,256]{1,0:T(8,128)S(1)}, u32[]{:S(2)}, u32[]{:S(2)}) %collective-permute-start.16) | collective-permute-done | bytes 524320 | tf_op jit(solution)/shard_map/ppermute | solution.py:299
  151.3 1.6 %shard_map.56 = f32[8,128,256]{2,1,0:T(8,128)} custom-call(s32[4]{0:T(128)S(1)} %pad_add_fusion.pos.refs_0_, f32[512,256]{1,0:T(8,128)S(1)} %pad_maximum_fusion.own, f32[512,256]{1,0:T(8,128)S(1)} %collective-permute-done.16.other), custom_call_target="tpu_custom_call" | custom-call | tf_op jit(solution)/shard_map/pallas_call | solution.py:42
  (3 shorter events, 0.1 us)
Async XLA Ops:
  12.2 7.2 %collective-permute-start = (f32[256,256]{1,0:T(8,128)S(1)}, f32[256,256]{1,0:T(8,128)S(1)}, u32[]{:S(2)}, u32[]{:S(2)}) collective-permute-start(f32[256,256]{1,0:T(8,128)S(1)} %get-tuple-element.17), channel_id=1, source_target_pairs={{0,64},{8,72},{16,80},{24,88},{32,96},{40,104},{48,112},{56,120},{... | collective-permute-start | bytes 786440 | tf_op jit(solution)/shard_map/ppermute | solution.py:277
  14.3 13.8 %collective-permute-start.1 = (f32[256,256]{1,0:T(8,128)S(1)}, f32[256,256]{1,0:T(8,128)S(1)}, u32[]{:S(2)}, u32[]{:S(2)}) collective-permute-start(f32[256,256]{1,0:T(8,128)S(1)} %get-tuple-element.18), channel_id=1, source_target_pairs={{0,128},{8,136},{16,144},{24,152},{32,160},{40,168},{48,176},{56,1... | collective-permute-start | bytes 786440 | tf_op jit(solution)/shard_map/ppermute | solution.py:277
  16.8 11.3 %collective-permute-start.2 = (f32[256,256]{1,0:T(8,128)S(1)}, f32[256,256]{1,0:T(8,128)S(1)}, u32[]{:S(2)}, u32[]{:S(2)}) collective-permute-start(f32[256,256]{1,0:T(8,128)S(1)} %get-tuple-element.19), channel_id=1, source_target_pairs={{0,192},{8,200},{16,208},{24,216},{32,224},{40,232},{48,240},{56,2... | collective-permute-start | bytes 786440 | tf_op jit(solution)/shard_map/ppermute | solution.py:277
  28.7 6.3 %collective-permute-start.3 = (f32[64,256]{1,0:T(8,128)S(1)}, f32[64,256]{1,0:T(8,128)S(1)}, u32[]{:S(2)}, u32[]{:S(2)}) collective-permute-start(f32[64,256]{1,0:T(8,128)S(1)} %get-tuple-element.21), channel_id=1, source_target_pairs={{0,16},{8,24},{16,0},{24,8},{32,48},{40,56},{48,32},{56,40},{64,80... | collective-permute-start | bytes 196616 | tf_op jit(solution)/shard_map/ppermute | solution.py:284
  31.8 5.6 %collective-permute-start.4 = (f32[64,256]{1,0:T(8,128)S(1)}, f32[64,256]{1,0:T(8,128)S(1)}, u32[]{:S(2)}, u32[]{:S(2)}) collective-permute-start(f32[64,256]{1,0:T(8,128)S(1)} %get-tuple-element.22), channel_id=1, source_target_pairs={{0,8},{8,16},{16,24},{24,0},{32,40},{40,48},{48,56},{56,32},{64,72... | collective-permute-start | bytes 196616 | tf_op jit(solution)/shard_map/ppermute | solution.py:284
  33.4 3.9 %collective-permute-start.5 = (f32[64,256]{1,0:T(8,128)S(1)}, f32[64,256]{1,0:T(8,128)S(1)}, u32[]{:S(2)}, u32[]{:S(2)}) collective-permute-start(f32[64,256]{1,0:T(8,128)S(1)} %get-tuple-element.23), channel_id=1, source_target_pairs={{0,24},{8,0},{16,8},{24,16},{32,56},{40,32},{48,40},{56,48},{64,88... | collective-permute-start | bytes 196616 | tf_op jit(solution)/shard_map/ppermute | solution.py:284
  37.4 7.7 %collective-permute-start.6 = (f32[64,256]{1,0:T(8,128)S(1)}, f32[64,256]{1,0:T(8,128)S(1)}, u32[]{:S(2)}, u32[]{:S(2)}) collective-permute-start(f32[64,256]{1,0:T(8,128)S(1)} %add_add_fusion), channel_id=1, source_target_pairs={{0,32},{8,40},{16,48},{24,56},{32,0},{40,8},{48,16},{56,24},{64,96... | collective-permute-start | bytes 196616 | tf_op jit(solution)/shard_map/ppermute | solution.py:289
  45.1 3.9 %collective-permute-start.9 = (f32[64,256]{1,0:T(8,128)S(1)}, f32[64,256]{1,0:T(8,128)S(1)}, u32[]{:S(2)}, u32[]{:S(2)}) collective-permute-start(f32[64,256]{1,0:T(8,128)S(1)} %add.26.a0), channel_id=1, source_target_pairs={{0,24},{8,0},{16,8},{24,16},{32,56},{40,32},{48,40},{56,48},{64,88... | collective-permute-start | bytes 196616 | tf_op jit(solution)/shard_map/ppermute | solution.py:284
  47.4 5.5 %collective-permute-start.8 = (f32[64,256]{1,0:T(8,128)S(1)}, f32[64,256]{1,0:T(8,128)S(1)}, u32[]{:S(2)}, u32[]{:S(2)}) collective-permute-start(f32[64,256]{1,0:T(8,128)S(1)} %add.26.a0), channel_id=1, source_target_pairs={{0,16},{8,24},{16,0},{24,8},{32,48},{40,56},{48,32},{56,40},{64,80... | collective-permute-start | bytes 196616 | tf_op jit(solution)/shard_map/ppermute | solution.py:284
  47.4 5.5 %collective-permute-start.7 = (f32[64,256]{1,0:T(8,128)S(1)}, f32[64,256]{1,0:T(8,128)S(1)}, u32[]{:S(2)}, u32[]{:S(2)}) collective-permute-start(f32[64,256]{1,0:T(8,128)S(1)} %add.26.a0), channel_id=1, source_target_pairs={{0,8},{8,16},{16,24},{24,0},{32,40},{40,48},{48,56},{56,32},{64,72... | collective-permute-start | bytes 196616 | tf_op jit(solution)/shard_map/ppermute | solution.py:284
  53.5 9.9 %collective-permute-start.12 = (f32[256,256]{1,0:T(8,128)S(1)}, f32[256,256]{1,0:T(8,128)S(1)}, u32[]{:S(2)}, u32[]{:S(2)}) collective-permute-start(f32[256,256]{1,0:T(8,128)S(1)} %shard_map.52.s0), channel_id=1, source_target_pairs={{0,192},{8,200},{16,208},{24,216},{32,224},{40,232},{48,240},{56,2... | collective-permute-start | bytes 786440 | tf_op jit(solution)/shard_map/ppermute | solution.py:277
  56.5 6.9 %collective-permute-start.11 = (f32[256,256]{1,0:T(8,128)S(1)}, f32[256,256]{1,0:T(8,128)S(1)}, u32[]{:S(2)}, u32[]{:S(2)}) collective-permute-start(f32[256,256]{1,0:T(8,128)S(1)} %shard_map.52.s0), channel_id=1, source_target_pairs={{0,128},{8,136},{16,144},{24,152},{32,160},{40,168},{48,176},{56,1... | collective-permute-start | bytes 786440 | tf_op jit(solution)/shard_map/ppermute | solution.py:277
  57.3 9.7 %collective-permute-start.10 = (f32[256,256]{1,0:T(8,128)S(1)}, f32[256,256]{1,0:T(8,128)S(1)}, u32[]{:S(2)}, u32[]{:S(2)}) collective-permute-start(f32[256,256]{1,0:T(8,128)S(1)} %shard_map.52.s0), channel_id=1, source_target_pairs={{0,64},{8,72},{16,80},{24,88},{32,96},{40,104},{48,112},{56,120},{... | collective-permute-start | bytes 786440 | tf_op jit(solution)/shard_map/ppermute | solution.py:277
  133.5 6.1 %collective-permute-start.15 = (f32[128,256]{1,0:T(8,128)S(1)}, f32[128,256]{1,0:T(8,128)S(1)}, u32[]{:S(2)}, u32[]{:S(2)}) collective-permute-start(f32[128,256]{1,0:T(8,128)S(1)} %shard_map.55), channel_id=1, source_target_pairs={{0,6},{1,7},{2,0},{3,1},{4,2},{5,3},{6,4},{7,5},{8,14},{9,15},{10,... | collective-permute-start | bytes 393224 | tf_op jit(solution)/shard_map/ppermute | solution.py:294
  136.2 5.4 %collective-permute-start.14 = (f32[128,256]{1,0:T(8,128)S(1)}, f32[128,256]{1,0:T(8,128)S(1)}, u32[]{:S(2)}, u32[]{:S(2)}) collective-permute-start(f32[128,256]{1,0:T(8,128)S(1)} %shard_map.55), channel_id=1, source_target_pairs={{0,4},{1,5},{2,6},{3,7},{4,0},{5,1},{6,2},{7,3},{8,12},{9,13},{10,... | collective-permute-start | bytes 393224 | tf_op jit(solution)/shard_map/ppermute | solution.py:294
  136.6 6.4 %collective-permute-start.13 = (f32[128,256]{1,0:T(8,128)S(1)}, f32[128,256]{1,0:T(8,128)S(1)}, u32[]{:S(2)}, u32[]{:S(2)}) collective-permute-start(f32[128,256]{1,0:T(8,128)S(1)} %shard_map.55), channel_id=1, source_target_pairs={{0,2},{1,3},{2,4},{3,5},{4,6},{5,7},{6,0},{7,1},{8,10},{9,11},{10,... | collective-permute-start | bytes 393224 | tf_op jit(solution)/shard_map/ppermute | solution.py:294
  143.0 8.3 %collective-permute-start.16 = (f32[512,256]{1,0:T(8,128)S(1)}, f32[512,256]{1,0:T(8,128)S(1)}, u32[]{:S(2)}, u32[]{:S(2)}) collective-permute-start(f32[512,256]{1,0:T(8,128)S(1)} %pad_maximum_fusion.own), channel_id=1, source_target_pairs={{0,1},{1,0},{2,3},{3,2},{4,5},{5,4},{6,7},{7,6},{8,9},{9,8},{10,11... | collective-permute-start | bytes 1572872 | tf_op jit(solution)/shard_map/ppermute | solution.py:299
